TPU v7x, 32 devices: a whole 2x2x4 slice. The times are simulated.
32 devices in a mesh: groups: 2 (over x), col: 16 (over z, y, core).
Axes of the slice: x: 2, y: 2, z: 4, core: 2. Of those that a mesh axis runs over, the one named last changes fastest.
Arguments:
- left_features: bfloat16 [32, 8, 8192], P(None, None, ('groups', 'col')), parts along dimension 2, may hold values from -3 to 3
- right_features: bfloat16 [32, 8, 8192], P(None, None, ('groups', 'col')), parts along dimension 2, may hold values from -3 to 3
- tile_offsets: int32 [32], P(('groups', 'col')), parts along dimension 0, may hold values from 0 to 3
- valid_mask: int32 [8, 8192], P(None, ('groups', 'col')), parts along dimension 1, may hold values 0 or 1
Outputs:
- disparity: float32 [8, 8192], P(None, ('groups', 'col')), parts along dimension 1
- final_volume: bfloat16 [192, 8, 8192], P(None, None, ('groups', 'col')), parts along dimension 2
There are 2 independent parts, one for each index of `groups`. A program takes and returns all parts, laid end to end along the dimension named above; each array names one. Nothing has to cross between parts.
All inputs are finite; a program needn't handle non-finite values. No bound on the sum of `valid_mask` on one device may be relied on, other than what follows from the above.
Results may differ from a plain program's by a relative error of at most 0.001.
Values may be sent and summed in bfloat16 or wider, within the bound.
A program may use at most 64 MiB of HBM per device.

v0:
```python
import functools
import math

import jax
import jax.numpy as jnp
from jax import lax
from jax.experimental import pallas as pl
from jax.experimental.pallas import tpu as pltpu
from jax.sharding import PartitionSpec as P

D = 192
ITERS = 4
FLOOR_COST = -4.0
LANES = 128
SUB = 8
MESH = pl.DeviceIdType.MESH
STEPS = tuple((a, b) for a in (-1, 0, 1) for b in (-1, 0, 1))
PITCH = D + 8
GROUP = 32
PER = LANES // GROUP
BLOCKS = D // PER


def lroll(x, shift):
    shift = shift % x.shape[-1]
    return x if shift == 0 else pltpu.roll(x, shift, x.ndim - 1)


def sroll(x, shift):
    shift = shift % x.shape[-2]
    return x if shift == 0 else pltpu.roll(x, shift, x.ndim - 2)


def iota(shape, dim):
    return lax.broadcasted_iota(jnp.int32, shape, dim)


def distances(plane):
    right = lroll(plane, -1)
    others = (right, sroll(plane, -1), sroll(right, -1), sroll(lroll(plane, 1), -1))
    return tuple((plane - other) ** 2 for other in others) + (plane * plane,)


def affinity(sums, channels):
    across, down, down_right, down_left, norm = sums
    row = iota(across.shape, 0)
    first, last = row == 0, row == across.shape[0] - 1
    dist = {(1, 0): across, (-1, 0): lroll(across, 1)}
    for a, base in ((1, down_right), (0, down), (-1, down_left)):
        dist[a, 1] = jnp.where(last, norm, base)
        dist[-a, -1] = jnp.where(first, norm, sroll(lroll(base, a), 1))
    e = {k: jnp.exp(-d / (2.0 * channels)) for k, d in dist.items()}
    e[0, 0] = jnp.ones_like(across)
    total = sum(e[k] for k in STEPS)
    out = {k: e[k] / total for k in STEPS}
    for a in (-1, 0, 1):
        out[a, 1] = jnp.where(last, 0.0, out[a, 1])
        out[a, -1] = jnp.where(first, 0.0, out[a, -1])
    return out


def coefficients(weights, usable, s1, s2):
    purity = D * s2 / (s1 * s1)
    gating = purity / (1.0 + purity)
    part = 0.25 * usable * (1.0 - gating)
    return {k: sroll(weights[k] * part, k[1]) for k in STEPS}, usable * gating


def stencil(w, left, mid, right):
    z = {}
    for b in (-1, 0, 1):
        z[b] = w[-1, b] * left + w[0, b] * mid + w[1, b] * right
    return z[0] + (sroll(z[1], -1) + sroll(z[-1], 1))


def pack(planes):
    lane = iota((SUB, LANES), 1)
    place = lane % GROUP
    out = jnp.zeros((SUB, LANES), jnp.float32)
    for s, (head, tail) in enumerate(planes):
        mine = lane // GROUP == s
        out = jnp.where(mine & (place >= 4) & (place < 16), lroll(head, GROUP * s + 4), out)
        out = jnp.where(mine & (place >= 16) & (place < 28), lroll(tail, GROUP * s + 16 - 116), out)
    return out


def kernel(
    n, left_ref, right_ref, offs_ref, mask_ref, disp_ref, vol_ref,
    prev, lf, rs, t4, u, v, own, sent, from_left, from_right, st, w_ref, send_sem, recv_sem,
):
    channels = left_ref.shape[0]
    tile = left_ref.shape[2]
    me = lax.axis_index("col")
    has_left, has_right = me > 0, me < n - 1
    lane = iota((SUB, LANES), 1)

    barrier = pltpu.get_barrier_semaphore()

    @pl.when(has_left)
    def _():
        pl.semaphore_signal(barrier, inc=1, device_id={"col": me - 1}, device_id_type=MESH)

    @pl.when(has_right)
    def _():
        pl.semaphore_signal(barrier, inc=1, device_id={"col": me + 1}, device_id_type=MESH)

    pl.semaphore_wait(barrier, has_left.astype(jnp.int32) + has_right.astype(jnp.int32))

    def remote(src, dst, slot, to):
        return pltpu.make_async_remote_copy(
            src_ref=src, dst_ref=dst, send_sem=send_sem.at[slot], recv_sem=recv_sem.at[slot],
            device_id={"col": to}, device_id_type=MESH,
        )

    tile_copy = remote(right_ref, prev, 0, me + 1)
    strip_right = remote(sent, from_left, 1, me + 1)
    strip_left = remote(sent, from_right, 2, me - 1)

    @pl.when(has_right)
    def _():
        tile_copy.start()

    @pl.when(jnp.logical_not(has_left))
    def _():
        prev[...] = jnp.zeros(prev.shape, prev.dtype)
        from_left[...] = jnp.zeros(from_left.shape, jnp.float32)

    @pl.when(jnp.logical_not(has_right))
    def _():
        from_right[...] = jnp.zeros(from_right.shape, jnp.float32)

    usable = mask_ref[...].astype(jnp.float32)

    zero = jnp.zeros((SUB, tile), jnp.float32)

    def channel(c, sums):
        plane = left_ref[c].astype(jnp.float32)
        at = pl.ds(pl.multiple_of(c * SUB, SUB), SUB)
        lf[0, at, :] = plane[:, :LANES]
        lf[1, at, :] = plane[:, LANES:]
        return tuple(s + d for s, d in zip(sums, distances(plane)))

    weights = affinity(lax.fori_loop(0, channels, channel, (zero,) * 5), channels)
    for i, k in enumerate(STEPS):
        w_ref[i] = weights[k]

    for q in range(channels // PER):
        planes = [
            (lf[0, (q * PER + s) * SUB : (q * PER + s + 1) * SUB, :],
             lf[1, (q * PER + s) * SUB : (q * PER + s + 1) * SUB, :])
            for s in range(PER)
        ]
        own[BLOCKS + q] = pack(planes)
    mask_at = BLOCKS + channels // PER
    own[mask_at] = pack([(usable[:, :LANES], usable[:, LANES:])] * PER)
    for q in range(mask_at + 1, own.shape[0]):
        own[q] = jnp.zeros((SUB, LANES), jnp.float32)

    @pl.when(has_left)
    def _():
        tile_copy.wait_recv()

    def shifts(c, carry):
        at = pl.ds(pl.multiple_of(c * SUB, SUB), SUB)
        before = prev[c].astype(jnp.float32)
        mine = right_ref[c].astype(jnp.float32)
        parts = (before[:, :LANES], before[:, LANES:], mine[:, :LANES], mine[:, LANES:])
        for s in range(4):
            rolled = [lroll(p, -s) for p in parts]
            for t in range(4):
                value = rolled[t]
                if s and t < 3:
                    value = jnp.where(lane < LANES - s, value, rolled[t + 1])
                rs[s, t, at, :] = value
        return carry

    lax.fori_loop(0, channels, shifts, 0)

    depth = 8 * channels
    keep = (iota((depth, tile), 0) // channels == iota((depth, tile), 1) % 8).astype(jnp.bfloat16)
    rows_out = tile - 8 + D
    begin = tile - D + 1

    def row(y, carry):
        for t in range(4):
            block = jnp.concatenate(
                [rs[s, t, pl.ds(y, channels, stride=SUB), :] for s in range(4)], axis=0
            )
            t4[t * LANES : (t + 1) * LANES, :] = block.T
        lhs = jnp.concatenate(
            [t4[begin : begin + rows_out, :], t4[begin + 4 : begin + 4 + rows_out, :]], axis=1
        ).astype(jnp.bfloat16)
        l_row = jnp.concatenate(
            [lf[t, pl.ds(y, channels, stride=SUB), :] for t in range(2)], axis=1
        ).astype(jnp.bfloat16)
        rhs = jnp.concatenate([l_row] * 8, axis=0) * keep
        scores = jnp.dot(lhs, rhs, preferred_element_type=jnp.float32)
        for t in range(2):
            x = scores[LANES * t : LANES * t + D + LANES - 8, LANES * t : LANES * (t + 1)]
            for bit in (64, 32, 16, 8):
                size = x.shape[0] - bit
                on = (iota((size, LANES), 1) // bit) % 2 == 1
                x = jnp.where(on, x[bit:], x[:size])
            u[t, pl.ds(pl.multiple_of(y * PITCH, 8), D), :] = x
        return carry

    lax.fori_loop(0, SUB, row, 0)

    scale = 1.0 / math.sqrt(channels)
    reach = offs_ref[0] * tile
    half = [usable[:, :LANES], usable[:, LANES:]]
    none = jnp.zeros((SUB, LANES), jnp.float32)

    def first(b, sums):
        sums = list(sums)
        planes = []
        for s in range(PER):
            j = b * PER + s
            pair = []
            for t in range(2):
                corr = u[t, pl.ds(j, SUB, stride=PITCH), :] * scale
                allowed = lane + (t * LANES) >= (D - 1 - j) - reach
                value = jnp.where(allowed, corr, FLOOR_COST) * half[t]
                v[t, j] = value
                e = jnp.exp(value)
                sums[2 * t] += e
                sums[2 * t + 1] += e * e
                pair.append(value)
            planes.append(pair)
        own[b] = pack(planes)
        return tuple(sums)

    sums = lax.fori_loop(0, BLOCKS, first, (none,) * 4)

    place4 = (lane % GROUP) // 4
    for m in range(sent.shape[0]):
        out = own[4 * m]
        for s, (p, q) in ((1, (3, 0)), (2, (5, 2)), (3, (7, 4))):
            out = jnp.where((place4 == p) | (place4 == q), lroll(own[4 * m + s], 8 * s), out)
        sent[m] = out

    @pl.when(has_right)
    def _():
        strip_right.start()

    @pl.when(has_left)
    def _():
        strip_left.start()

    head_lane, tail_lane = lane == 0, lane == LANES - 1
    UN = PER

    def step(sums, last):
        coef = []
        for t in range(2):
            cols = slice(t * LANES, (t + 1) * LANES)
            coef.append(
                coefficients(
                    {k: w_ref[i, :, cols] for i, k in enumerate(STEPS)},
                    half[t], sums[2 * t], sums[2 * t + 1],
                )
            )

        def pooled(j):
            mid = (v[0, j], v[1, j])
            r = [lroll(m, 1) for m in mid]
            l = [lroll(m, -1) for m in mid]
            lefts = (r[0], jnp.where(head_lane, r[0], r[1]))
            rights = (jnp.where(tail_lane, l[1], l[0]), l[1])
            return [stencil(coef[t][0], lefts[t], mid[t], rights[t]) for t in range(2)], mid

        def finish(j, pair, sums, strip, s):
            sums = list(sums)
            if last:
                pair = list(pair)
                pair[0] = jnp.where(lane < 4, lroll(strip, -(GROUP * s + 4)), pair[0])
                pair[1] = jnp.where(lane >= LANES - 4, lroll(strip, 100 - GROUP * s), pair[1])
                vol_ref[D - 1 - j] = jnp.concatenate(pair, axis=1).astype(jnp.bfloat16)
                level = (D - 1 - j).astype(jnp.float32) * (1.0 / D)
            for t in range(2):
                if not last:
                    v[t, j] = pair[t]
                e = jnp.exp(pair[t])
                sums[2 * t] += e
                sums[2 * t + 1] += e * level if last else e * e
            return tuple(sums)

        def block(b, carry):
            p_prev, s_prev, v_prev, sums = carry
            for s in range(UN):
                j = b * UN + s
                p, mid = pooled(j)
                s_now = [p_prev[t] + p[t] for t in range(2)]
                new = [coef[t][1] * v_prev[t] + (s_prev[t] + s_now[t]) for t in range(2)]
                q = (s - 1) % PER
                strip = st[b - 1 if s == 0 else b] if last else None
                sums = finish(j - 1, new, sums, strip, q)
                p_prev, s_prev, v_prev = p, s_now, mid
            return p_prev, s_prev, v_prev, sums

        p0, mid0 = pooled(0)
        carry = (p0, [2.0 * p for p in p0], list(mid0), (none,) * 4)
        p_prev, s_prev, v_prev, acc = carry
        for s in range(1, UN):
            p, mid = pooled(s)
            s_now = [p_prev[t] + p[t] for t in range(2)]
            new = [coef[t][1] * v_prev[t] + (s_prev[t] + s_now[t]) for t in range(2)]
            acc = finish(jnp.int32(s - 1), new, acc, st[0] if last else None, s - 1)
            p_prev, s_prev, v_prev = p, s_now, list(mid)
        carry = (tuple(p_prev), tuple(s_prev), tuple(v_prev), acc)

        def loop(b, carry):
            p, s, m, acc = block(b, carry)
            return tuple(p), tuple(s), tuple(m), acc

        p_prev, s_prev, v_prev, acc = lax.fori_loop(1, D // UN, loop, carry)
        new = [
            coef[t][1] * v_prev[t] + (s_prev[t] + 2.0 * p_prev[t]) for t in range(2)
        ]
        return finish(jnp.int32(D - 1), new, acc, st[BLOCKS - 1] if last else None, PER - 1)

    sums = lax.fori_loop(0, ITERS - 1, lambda i, s: step(s, False), sums)

    @pl.when(has_left)
    def _():
        strip_right.wait_recv()

    @pl.when(has_right)
    def _():
        strip_left.wait_recv()

    place = lane % GROUP

    def joined(m, s):
        out = jnp.where(place < 4, lroll(from_left[m], -24 - 8 * s), own[4 * m + s])
        return jnp.where(place >= 28, lroll(from_right[m], 24 - 8 * s), out)

    def over_groups(x):
        x = x + lroll(x, GROUP)
        return x + lroll(x, 2 * GROUP)

    s1, s2 = none, none
    for m in range(BLOCKS // 4):
        for s in range(4):
            value = joined(m, s)
            st[4 * m + s] = value
            e = jnp.exp(value)
            s1, s2 = s1 + e, s2 + e * e
    strip_sums = (none,) * 5
    for q in range(channels // PER):
        at = BLOCKS + q
        strip_sums = [
            a + d for a, d in zip(strip_sums, distances(joined(at // 4, at % 4)))
        ]
    strip_weights = affinity([over_groups(x) for x in strip_sums], channels)
    strip_usable = joined(mask_at // 4, mask_at % 4)
    low, high = lane < GROUP, lane >= LANES - GROUP

    def strip_step(i, sums):
        s1, s2 = sums
        w, keep_own = coefficients(strip_weights, strip_usable, over_groups(s1), over_groups(s2))
        s1, s2 = none, none

        def pooled(value):
            p = stencil(w, lroll(value, 1), value, lroll(value, -1))
            return p, lroll(p, GROUP), lroll(p, -GROUP)

        value = st[0]
        p, up, down = pooled(value)
        lower = jnp.where(low, p, up)
        for b in range(BLOCKS):
            if b + 1 < BLOCKS:
                value_next = st[b + 1]
                p_next, up_next, down_next = pooled(value_next)
                upper = jnp.where(high, down_next, down)
            else:
                upper = jnp.where(high, p, down)
            new = keep_own * value + ((lower + upper) + 2.0 * p)
            st[b] = new
            e = jnp.exp(new)
            s1, s2 = s1 + e, s2 + e * e
            if b + 1 < BLOCKS:
                lower = jnp.where(low, up, up_next)
                value, p, up, down = value_next, p_next, up_next, down_next
        return s1, s2

    lax.fori_loop(0, ITERS, strip_step, (s1, s2))

    out = step(sums, True)
    for t in range(2):
        disp_ref[:, t * LANES : (t + 1) * LANES] = out[2 * t + 1] / out[2 * t]

    @pl.when(has_right)
    def _():
        tile_copy.wait_send()
        strip_right.wait_send()

    @pl.when(has_left)
    def _():
        strip_left.wait_send()


def on_device(n, left_features, right_features, tile_offsets, valid_mask):
    channels, rows, tile = left_features.shape
    vmem = pl.BlockSpec(memory_space=pltpu.VMEM)
    strips = -(-(BLOCKS + channels // PER + 1) // 4) * 4
    f32 = jnp.float32
    return pl.pallas_call(
        functools.partial(kernel, n),
        out_shape=(
            jax.ShapeDtypeStruct((rows, tile), f32),
            jax.ShapeDtypeStruct((D, rows, tile), jnp.bfloat16),
        ),
        in_specs=[vmem, vmem, pl.BlockSpec(memory_space=pltpu.SMEM), vmem],
        out_specs=(vmem, vmem),
        scratch_shapes=[
            pltpu.VMEM((channels, rows, tile), jnp.bfloat16),
            pltpu.VMEM((2, channels * SUB, LANES), f32),
            pltpu.VMEM((4, 4, channels * SUB, LANES), f32),
            pltpu.VMEM((2 * tile, LANES), f32),
            pltpu.VMEM((2, SUB * PITCH, LANES), f32),
            pltpu.VMEM((2, D, SUB, LANES), f32),
            pltpu.VMEM((strips, SUB, LANES), f32),
            pltpu.VMEM((strips // 4, SUB, LANES), f32),
            pltpu.VMEM((strips // 4, SUB, LANES), f32),
            pltpu.VMEM((strips // 4, SUB, LANES), f32),
            pltpu.VMEM((BLOCKS, SUB, LANES), f32),
            pltpu.VMEM((len(STEPS), SUB, tile), f32),
            pltpu.SemaphoreType.DMA((3,)),
            pltpu.SemaphoreType.DMA((3,)),
        ],
        compiler_params=pltpu.CompilerParams(collective_id=0, has_side_effects=True),
    )(left_features, right_features, tile_offsets, valid_mask)


def solution(mesh):
    return jax.shard_map(
        functools.partial(on_device, mesh.shape["col"]),
        mesh=mesh,
        in_specs=(
            P(None, None, ("groups", "col")),
            P(None, None, ("groups", "col")),
            P(("groups", "col")),
            P(None, ("groups", "col")),
        ),
        out_specs=(P(None, ("groups", "col")), P(None, None, ("groups", "col"))),
        check_vma=False,
    )
```

profile of v0, /device:TPU:24, one launch (start us, length us, event | category | flops | bytes accessed | tf_op | source)
XLA Modules:
  0.0 44.2 jit_solution(17446189769657079083)
XLA Ops:
  1.3 39.5 %shard_map.59 = (f32[8,256]{1,0:T(8,128)}, bf16[192,8,256]{2,1,0:T(8,128)(2,1)}) custom-call(bf16[32,8,256]{2,1,0:T(8,128)(2,1)} %left_ref.1, bf16[32,8,256]{2,1,0:T(8,128)(2,1)} %right_ref.1, s32[1]{0:T(128)S(6)} %copy.8.offs_ref, s32[8,256]{1,0:T(8,128)} %mask_ref.1), custom_call_target="tpu_custom_call" | custom-call | tf_op jit(solution)/shard_map/pallas_call | solution.py:408
  40.8 1.3 %copy.9 = f32[8,256]{1,0:T(8,128)} copy(f32[8,256]{1,0:T(8,128)} %get-tuple-element.4) | data formatting | bytes 16384
  42.1 2.1 %copy.10 = bf16[192,8,256]{2,1,0:T(8,128)(2,1)} copy(bf16[192,8,256]{2,1,0:T(8,128)(2,1)} %get-tuple-element.5) | data formatting | bytes 1572864
where the time goes:
time: 44.4 us; the launch traced here: 44.2 us
  Pallas kernels  39.5 us (89%)
  local copies, waits for them, and re-layouts  3.36 us (8%)
  between operations  1.28 us (3%)
    pallas_call x1, Pallas kernels, on_device(): pl.pallas_call(functools.partial(kernel, n), out_shape=(jax.ShapeDtypeStr...  39.5 us
    unnamed x2, local copies, waits for them, and re-layouts  3.36 us

commit v1 on v0

--- a/solution.py
+++ b/solution.py
@@ -19,6 +19,11 @@
 GROUP = 32
 PER = LANES // GROUP
 BLOCKS = D // PER
+LOG2E = math.log2(math.e)
+FIRST_UNROLL = 4
+UNROLL = 8
+STRIP_UNROLL = 8
+ROW_UNROLL = 2
 
 
 def lroll(x, shift):
@@ -63,14 +68,16 @@
     purity = D * s2 / (s1 * s1)
     gating = purity / (1.0 + purity)
     part = 0.25 * usable * (1.0 - gating)
-    return {k: sroll(weights[k] * part, k[1]) for k in STEPS}, usable * gating
-
-
-def stencil(w, left, mid, right):
-    z = {}
-    for b in (-1, 0, 1):
-        z[b] = w[-1, b] * left + w[0, b] * mid + w[1, b] * right
-    return z[0] + (sroll(z[1], -1) + sroll(z[-1], 1))
+    return {k: lroll(weights[k] * part, k[0]) for k in STEPS}, usable * gating
+
+
+def columns(w, above, mid, below):
+    return [w[a, -1] * above + w[a, 0] * mid + w[a, 1] * below for a in (-1, 0, 1)]
+
+
+def three(ref, s):
+    at = (s + 1) * SUB
+    return ref[at - 1 : at - 1 + SUB, :], ref[at : at + SUB, :], ref[at + 1 : at + 1 + SUB, :]
 
 
 def pack(planes):
@@ -181,56 +188,68 @@
     rows_out = tile - 8 + D
     begin = tile - D + 1
 
-    def row(y, carry):
-        for t in range(4):
-            block = jnp.concatenate(
-                [rs[s, t, pl.ds(y, channels, stride=SUB), :] for s in range(4)], axis=0
-            )
-            t4[t * LANES : (t + 1) * LANES, :] = block.T
-        lhs = jnp.concatenate(
-            [t4[begin : begin + rows_out, :], t4[begin + 4 : begin + 4 + rows_out, :]], axis=1
-        ).astype(jnp.bfloat16)
-        l_row = jnp.concatenate(
-            [lf[t, pl.ds(y, channels, stride=SUB), :] for t in range(2)], axis=1
-        ).astype(jnp.bfloat16)
-        rhs = jnp.concatenate([l_row] * 8, axis=0) * keep
-        scores = jnp.dot(lhs, rhs, preferred_element_type=jnp.float32)
-        for t in range(2):
-            x = scores[LANES * t : LANES * t + D + LANES - 8, LANES * t : LANES * (t + 1)]
-            for bit in (64, 32, 16, 8):
-                size = x.shape[0] - bit
-                on = (iota((size, LANES), 1) // bit) % 2 == 1
-                x = jnp.where(on, x[bit:], x[:size])
-            u[t, pl.ds(pl.multiple_of(y * PITCH, 8), D), :] = x
+    def row(i, carry):
+        for h in range(ROW_UNROLL):
+            y = i * ROW_UNROLL + h
+            for t in range(4):
+                block = jnp.concatenate(
+                    [rs[s, t, pl.ds(y, channels, stride=SUB), :] for s in range(4)], axis=0
+                )
+                t4[h, t * LANES : (t + 1) * LANES, :] = block.T
+        for h in range(ROW_UNROLL):
+            y = i * ROW_UNROLL + h
+            lhs = jnp.concatenate(
+                [t4[h, begin : begin + rows_out, :], t4[h, begin + 4 : begin + 4 + rows_out, :]],
+                axis=1,
+            ).astype(jnp.bfloat16)
+            l_row = jnp.concatenate(
+                [lf[t, pl.ds(y, channels, stride=SUB), :] for t in range(2)], axis=1
+            ).astype(jnp.bfloat16)
+            rhs = jnp.concatenate([l_row] * 8, axis=0) * keep
+            scores = jnp.dot(lhs, rhs, preferred_element_type=jnp.float32)
+            for t in range(2):
+                x = scores[LANES * t : LANES * t + D + LANES - 8, LANES * t : LANES * (t + 1)]
+                for bit in (64, 32, 16, 8):
+                    size = x.shape[0] - bit
+                    on = (iota((size, LANES), 1) // bit) % 2 == 1
+                    x = jnp.where(on, x[bit:], x[:size])
+                u[t, pl.ds(pl.multiple_of(y * PITCH, 8), D), :] = x
         return carry
 
-    lax.fori_loop(0, SUB, row, 0)
-
-    scale = 1.0 / math.sqrt(channels)
+    lax.fori_loop(0, SUB // ROW_UNROLL, row, 0)
+
+    scale = LOG2E / math.sqrt(channels)
     reach = offs_ref[0] * tile
     half = [usable[:, :LANES], usable[:, LANES:]]
     none = jnp.zeros((SUB, LANES), jnp.float32)
-
-    def first(b, sums):
+    for t in range(2):
+        v[t, :SUB, :] = none
+        v[t, (D + 1) * SUB :, :] = none
+    st[:SUB, :] = none
+    st[(BLOCKS + 1) * SUB :, :] = none
+
+    def first(i, sums):
         sums = list(sums)
-        planes = []
-        for s in range(PER):
-            j = b * PER + s
-            pair = []
-            for t in range(2):
-                corr = u[t, pl.ds(j, SUB, stride=PITCH), :] * scale
-                allowed = lane + (t * LANES) >= (D - 1 - j) - reach
-                value = jnp.where(allowed, corr, FLOOR_COST) * half[t]
-                v[t, j] = value
-                e = jnp.exp(value)
-                sums[2 * t] += e
-                sums[2 * t + 1] += e * e
-                pair.append(value)
-            planes.append(pair)
-        own[b] = pack(planes)
+        for h in range(FIRST_UNROLL):
+            b = i * FIRST_UNROLL + h
+            planes = []
+            for s in range(PER):
+                j = b * PER + s
+                pair = []
+                for t in range(2):
+                    corr = u[t, pl.ds(j, SUB, stride=PITCH), :] * scale
+                    allowed = lane >= (D - 1 - j) - reach - t * LANES
+                    value = jnp.where(allowed, corr, FLOOR_COST * LOG2E) * half[t]
+                    v[t, pl.ds(pl.multiple_of((j + 1) * SUB, SUB), SUB), :] = value
+                    e = jnp.exp2(value)
+                    sums[2 * t] += e
+                    sums[2 * t + 1] += e * e
+                    pair.append(value)
+                planes.append(pair)
+            own[b] = pack(planes)
         return tuple(sums)
 
-    sums = lax.fori_loop(0, BLOCKS, first, (none,) * 4)
+    sums = lax.fori_loop(0, BLOCKS // FIRST_UNROLL, first, (none,) * 4)
 
     place4 = (lane % GROUP) // 4
     for m in range(sent.shape[0]):
@@ -248,76 +267,78 @@
         strip_left.start()
 
     head_lane, tail_lane = lane == 0, lane == LANES - 1
-    UN = PER
 
     def step(sums, last):
-        coef = []
-        for t in range(2):
-            cols = slice(t * LANES, (t + 1) * LANES)
-            coef.append(
-                coefficients(
-                    {k: w_ref[i, :, cols] for i, k in enumerate(STEPS)},
-                    half[t], sums[2 * t], sums[2 * t + 1],
-                )
-            )
-
-        def pooled(j):
-            mid = (v[0, j], v[1, j])
-            r = [lroll(m, 1) for m in mid]
-            l = [lroll(m, -1) for m in mid]
-            lefts = (r[0], jnp.where(head_lane, r[0], r[1]))
-            rights = (jnp.where(tail_lane, l[1], l[0]), l[1])
-            return [stencil(coef[t][0], lefts[t], mid[t], rights[t]) for t in range(2)], mid
-
-        def finish(j, pair, sums, strip, s):
-            sums = list(sums)
+        wide = lambda a, b: jnp.concatenate([a, b], axis=1)
+        w, keep_own = coefficients(
+            {k: w_ref[i] for i, k in enumerate(STEPS)}, usable,
+            wide(sums[0], sums[2]), wide(sums[1], sums[3]),
+        )
+        cut = lambda x, t: x[:, t * LANES : (t + 1) * LANES]
+        w = [{k: cut(w[k], t) for k in STEPS} for t in range(2)]
+        keep_own = [cut(keep_own, t) for t in range(2)]
+
+        def pooled(refs, s):
+            z, mid = [], []
+            for t in range(2):
+                rows = three(refs[t], s)
+                mid.append(rows[1])
+                z.append(columns(w[t], *rows))
+            r = [lroll(z[t][0], 1) for t in range(2)]
+            l = [lroll(z[t][2], -1) for t in range(2)]
+            r[1] = jnp.where(head_lane, r[0], r[1])
+            l[0] = jnp.where(tail_lane, l[1], l[0])
+            return [z[t][1] + (r[t] + l[t]) for t in range(2)], mid
+
+        def finish(b, s, pair, sums):
+            j = b * UNROLL + s
+            pair, sums = list(pair), list(sums)
             if last:
-                pair = list(pair)
-                pair[0] = jnp.where(lane < 4, lroll(strip, -(GROUP * s + 4)), pair[0])
-                pair[1] = jnp.where(lane >= LANES - 4, lroll(strip, 100 - GROUP * s), pair[1])
-                vol_ref[D - 1 - j] = jnp.concatenate(pair, axis=1).astype(jnp.bfloat16)
+                group = s % PER
+                row = pl.multiple_of((b * (UNROLL // PER) + s // PER + 1) * SUB, SUB)
+                strip = st[pl.ds(row, SUB), :]
+                pair[0] = jnp.where(lane < 4, lroll(strip, -(GROUP * group + 4)), pair[0])
+                pair[1] = jnp.where(lane >= LANES - 4, lroll(strip, 100 - GROUP * group), pair[1])
+                out = jnp.concatenate(pair, axis=1) * (1.0 / LOG2E)
+                vol_ref[D - 1 - j] = out.astype(jnp.bfloat16)
                 level = (D - 1 - j).astype(jnp.float32) * (1.0 / D)
             for t in range(2):
                 if not last:
-                    v[t, j] = pair[t]
-                e = jnp.exp(pair[t])
+                    v[t, pl.ds(pl.multiple_of((j + 1) * SUB, SUB), SUB), :] = pair[t]
+                e = jnp.exp2(pair[t])
                 sums[2 * t] += e
-                sums[2 * t + 1] += e * level if last else e * e
-            return tuple(sums)
-
-        def block(b, carry):
-            p_prev, s_prev, v_prev, sums = carry
-            for s in range(UN):
-                j = b * UN + s
-                p, mid = pooled(j)
-                s_now = [p_prev[t] + p[t] for t in range(2)]
-                new = [coef[t][1] * v_prev[t] + (s_prev[t] + s_now[t]) for t in range(2)]
-                q = (s - 1) % PER
-                strip = st[b - 1 if s == 0 else b] if last else None
-                sums = finish(j - 1, new, sums, strip, q)
-                p_prev, s_prev, v_prev = p, s_now, mid
-            return p_prev, s_prev, v_prev, sums
-
-        p0, mid0 = pooled(0)
-        carry = (p0, [2.0 * p for p in p0], list(mid0), (none,) * 4)
-        p_prev, s_prev, v_prev, acc = carry
-        for s in range(1, UN):
-            p, mid = pooled(s)
+                sums[2 * t + 1] += e * (level if last else e)
+            return sums
+
+        def advance(refs, b, s, carry):
+            p_prev, s_prev, v_prev, acc = carry
+            p, mid = pooled(refs, s)
             s_now = [p_prev[t] + p[t] for t in range(2)]
-            new = [coef[t][1] * v_prev[t] + (s_prev[t] + s_now[t]) for t in range(2)]
-            acc = finish(jnp.int32(s - 1), new, acc, st[0] if last else None, s - 1)
-            p_prev, s_prev, v_prev = p, s_now, list(mid)
-        carry = (tuple(p_prev), tuple(s_prev), tuple(v_prev), acc)
+            new = [keep_own[t] * v_prev[t] + (s_prev[t] + s_now[t]) for t in range(2)]
+            before = (b - 1, UNROLL - 1) if s == 0 else (b, s - 1)
+            return p, s_now, mid, finish(*before, new, acc)
+
+        def block_refs(b):
+            at = pl.ds(pl.multiple_of(b * (UNROLL * SUB), SUB), (UNROLL + 2) * SUB)
+            return [v.at[t, at, :] for t in range(2)]
 
         def loop(b, carry):
-            p, s, m, acc = block(b, carry)
-            return tuple(p), tuple(s), tuple(m), acc
-
-        p_prev, s_prev, v_prev, acc = lax.fori_loop(1, D // UN, loop, carry)
-        new = [
-            coef[t][1] * v_prev[t] + (s_prev[t] + 2.0 * p_prev[t]) for t in range(2)
-        ]
-        return finish(jnp.int32(D - 1), new, acc, st[BLOCKS - 1] if last else None, PER - 1)
+            p, s, m, acc = carry
+            carry = list(p), list(s), list(m), list(acc)
+            refs = block_refs(b)
+            for k in range(UNROLL):
+                carry = advance(refs, b, k, carry)
+            return tuple(tuple(c) for c in carry)
+
+        refs = block_refs(0)
+        p, mid = pooled(refs, 0)
+        carry = p, [2.0 * x for x in p], mid, [none] * 4
+        for k in range(1, UNROLL):
+            carry = advance(refs, jnp.int32(0), k, carry)
+        carry = tuple(tuple(c) for c in carry)
+        p_prev, s_prev, v_prev, acc = lax.fori_loop(1, D // UNROLL, loop, carry)
+        new = [keep_own[t] * v_prev[t] + (s_prev[t] + 2.0 * p_prev[t]) for t in range(2)]
+        return tuple(finish(jnp.int32(D // UNROLL - 1), UNROLL - 1, new, acc))
 
     sums = lax.fori_loop(0, ITERS - 1, lambda i, s: step(s, False), sums)
 
@@ -343,8 +364,8 @@
     for m in range(BLOCKS // 4):
         for s in range(4):
             value = joined(m, s)
-            st[4 * m + s] = value
-            e = jnp.exp(value)
+            st[(4 * m + s + 1) * SUB : (4 * m + s + 2) * SUB, :] = value
+            e = jnp.exp2(value)
             s1, s2 = s1 + e, s2 + e * e
     strip_sums = (none,) * 5
     for q in range(channels // PER):
@@ -357,32 +378,46 @@
     low, high = lane < GROUP, lane >= LANES - GROUP
 
     def strip_step(i, sums):
-        s1, s2 = sums
-        w, keep_own = coefficients(strip_weights, strip_usable, over_groups(s1), over_groups(s2))
-        s1, s2 = none, none
-
-        def pooled(value):
-            p = stencil(w, lroll(value, 1), value, lroll(value, -1))
-            return p, lroll(p, GROUP), lroll(p, -GROUP)
-
-        value = st[0]
-        p, up, down = pooled(value)
-        lower = jnp.where(low, p, up)
-        for b in range(BLOCKS):
-            if b + 1 < BLOCKS:
-                value_next = st[b + 1]
-                p_next, up_next, down_next = pooled(value_next)
-                upper = jnp.where(high, down_next, down)
-            else:
-                upper = jnp.where(high, p, down)
+        w, keep_own = coefficients(
+            strip_weights, strip_usable, over_groups(sums[0]), over_groups(sums[1])
+        )
+
+        def pooled(ref, s):
+            rows = three(ref, s)
+            z = columns(w, *rows)
+            p = z[1] + (lroll(z[0], 1) + lroll(z[2], -1))
+            return p, lroll(p, GROUP), lroll(p, -GROUP), rows[1]
+
+        def finish(b, p, up, before, down, after, value, acc):
+            lower, upper = jnp.where(low, before, up), jnp.where(high, after, down)
             new = keep_own * value + ((lower + upper) + 2.0 * p)
-            st[b] = new
-            e = jnp.exp(new)
-            s1, s2 = s1 + e, s2 + e * e
-            if b + 1 < BLOCKS:
-                lower = jnp.where(low, up, up_next)
-                value, p, up, down = value_next, p_next, up_next, down_next
-        return s1, s2
+            st[pl.ds(pl.multiple_of((b + 1) * SUB, SUB), SUB), :] = new
+            e = jnp.exp2(new)
+            return acc[0] + e, acc[1] + e * e
+
+        def advance(ref, b, s, carry):
+            p, up, down, before, value, acc = carry
+            p_now, up_now, down_now, value_now = pooled(ref, s)
+            acc = finish(b * STRIP_UNROLL + s - 1, p, up, before, down, down_now, value, acc)
+            return p_now, up_now, down_now, up, value_now, acc
+
+        def block_ref(b):
+            at = pl.ds(pl.multiple_of(b * (STRIP_UNROLL * SUB), SUB), (STRIP_UNROLL + 2) * SUB)
+            return st.at[at, :]
+
+        def loop(b, carry):
+            ref = block_ref(b)
+            for k in range(STRIP_UNROLL):
+                carry = advance(ref, b, k, carry)
+            return carry
+
+        ref = block_ref(0)
+        p, up, down, value = pooled(ref, 0)
+        carry = p, up, down, p, value, (none, none)
+        for k in range(1, STRIP_UNROLL):
+            carry = advance(ref, jnp.int32(0), k, carry)
+        p, up, down, before, value, acc = lax.fori_loop(1, BLOCKS // STRIP_UNROLL, loop, carry)
+        return finish(jnp.int32(BLOCKS - 1), p, up, before, down, p, value, acc)
 
     lax.fori_loop(0, ITERS, strip_step, (s1, s2))
 
@@ -417,14 +452,14 @@
             pltpu.VMEM((channels, rows, tile), jnp.bfloat16),
             pltpu.VMEM((2, channels * SUB, LANES), f32),
             pltpu.VMEM((4, 4, channels * SUB, LANES), f32),
-            pltpu.VMEM((2 * tile, LANES), f32),
+            pltpu.VMEM((ROW_UNROLL, 2 * tile, LANES), f32),
             pltpu.VMEM((2, SUB * PITCH, LANES), f32),
-            pltpu.VMEM((2, D, SUB, LANES), f32),
+            pltpu.VMEM((2, (D + 2) * SUB, LANES), f32),
             pltpu.VMEM((strips, SUB, LANES), f32),
             pltpu.VMEM((strips // 4, SUB, LANES), f32),
             pltpu.VMEM((strips // 4, SUB, LANES), f32),
             pltpu.VMEM((strips // 4, SUB, LANES), f32),
-            pltpu.VMEM((BLOCKS, SUB, LANES), f32),
+            pltpu.VMEM(((BLOCKS + 2) * SUB, LANES), f32),
             pltpu.VMEM((len(STEPS), SUB, tile), f32),
             pltpu.SemaphoreType.DMA((3,)),
             pltpu.SemaphoreType.DMA((3,)),

time: 44.4 us -> 40.5 us (0.912)
  Pallas kernels: 39.5 us -> 35.6 us
    pallas_call x1, Pallas kernels: 39.5 us -> 35.6 us  [on_device(): pl.pallas_call(functools.partial(kernel, n), out_shape=(jax.ShapeDtypeStr...]
where the time goes in v1:
time: 40.5 us; the launch traced here: 40.2 us
  Pallas kernels  35.6 us (88%)
  local copies, waits for them, and re-layouts  3.36 us (8%)
  between operations  1.28 us (3%)
    pallas_call x1, Pallas kernels, on_device(): pl.pallas_call(functools.partial(kernel, n), out_shape=(jax.ShapeDtypeStr...  35.6 us
    unnamed x2, local copies, waits for them, and re-layouts  3.36 us

profile of v1, /device:TPU:24, one launch (start us, length us, event | category | flops | bytes accessed | tf_op | source)
XLA Modules:
  0.0 40.2 jit_solution(5441890952797900275)
XLA Ops:
  1.3 35.6 %shard_map.59 = (f32[8,256]{1,0:T(8,128)}, bf16[192,8,256]{2,1,0:T(8,128)(2,1)}) custom-call(bf16[32,8,256]{2,1,0:T(8,128)(2,1)} %left_ref.1, bf16[32,8,256]{2,1,0:T(8,128)(2,1)} %right_ref.1, s32[1]{0:T(128)S(6)} %copy.8.offs_ref, s32[8,256]{1,0:T(8,128)} %mask_ref.1), custom_call_target="tpu_custom_call" | custom-call | tf_op jit(solution)/shard_map/pallas_call | solution.py:443
  36.9 1.3 %copy.9 = f32[8,256]{1,0:T(8,128)} copy(f32[8,256]{1,0:T(8,128)} %get-tuple-element.4) | data formatting | bytes 16384
  38.2 2.1 %copy.10 = bf16[192,8,256]{2,1,0:T(8,128)(2,1)} copy(bf16[192,8,256]{2,1,0:T(8,128)(2,1)} %get-tuple-element.5) | data formatting | bytes 1572864

commit v2 on v1

--- a/solution.py
+++ b/solution.py
@@ -20,10 +20,10 @@
 PER = LANES // GROUP
 BLOCKS = D // PER
 LOG2E = math.log2(math.e)
-FIRST_UNROLL = 4
-UNROLL = 8
-STRIP_UNROLL = 8
-ROW_UNROLL = 2
+FIRST_UNROLL = 48
+UNROLL = 96
+STRIP_UNROLL = 48
+ROW_UNROLL = 4
 
 
 def lroll(x, shift):

time: 40.5 us -> 24.8 us (0.61)
  Pallas kernels: 35.6 us -> 19.9 us
    pallas_call x1, Pallas kernels: 35.6 us -> 19.9 us  [on_device(): pl.pallas_call(functools.partial(kernel, n), out_shape=(jax.ShapeDtypeStr...]
where the time goes in v2:
time: 24.8 us; the launch traced here: 24.6 us
  Pallas kernels  19.9 us (80%)
  local copies, waits for them, and re-layouts  3.36 us (14%)
  between operations  1.28 us (5%)
    pallas_call x1, Pallas kernels, on_device(): pl.pallas_call(functools.partial(kernel, n), out_shape=(jax.ShapeDtypeStr...  19.9 us
    unnamed x2, local copies, waits for them, and re-layouts  3.36 us

profile of v2, /device:TPU:24, one launch (start us, length us, event | category | flops | bytes accessed | tf_op | source)
XLA Modules:
  0.0 24.6 jit_solution(17549777294924039408)
XLA Ops:
  1.3 19.9 %shard_map.59 = (f32[8,256]{1,0:T(8,128)}, bf16[192,8,256]{2,1,0:T(8,128)(2,1)}) custom-call(bf16[32,8,256]{2,1,0:T(8,128)(2,1)} %left_ref.1, bf16[32,8,256]{2,1,0:T(8,128)(2,1)} %right_ref.1, s32[1]{0:T(128)S(6)} %copy.8.offs_ref, s32[8,256]{1,0:T(8,128)} %mask_ref.1), custom_call_target="tpu_custom_call" | custom-call | tf_op jit(solution)/shard_map/pallas_call | solution.py:443
  21.2 1.3 %copy.9 = f32[8,256]{1,0:T(8,128)} copy(f32[8,256]{1,0:T(8,128)} %get-tuple-element.4) | data formatting | bytes 16384
  22.5 2.1 %copy.10 = bf16[192,8,256]{2,1,0:T(8,128)(2,1)} copy(bf16[192,8,256]{2,1,0:T(8,128)(2,1)} %get-tuple-element.5) | data formatting | bytes 1572864

commit v3 on v2

--- a/solution.py
+++ b/solution.py
@@ -24,6 +24,8 @@
 UNROLL = 96
 STRIP_UNROLL = 48
 ROW_UNROLL = 4
+CHANNEL_UNROLL = 8
+VMEM_LIMIT = 24 * 1024 * 1024
 
 
 def lroll(x, shift):
@@ -91,9 +93,86 @@
     return out
 
 
+def step(v, st, w_ref, usable, vol_ref, sums):
+    last = vol_ref is not None
+    lane = iota((SUB, LANES), 1)
+    head_lane, tail_lane = lane == 0, lane == LANES - 1
+    none = jnp.zeros((SUB, LANES), jnp.float32)
+    wide = lambda a, b: jnp.concatenate([a, b], axis=1)
+    w, keep_own = coefficients(
+        {k: w_ref[i] for i, k in enumerate(STEPS)}, usable,
+        wide(sums[0], sums[2]), wide(sums[1], sums[3]),
+    )
+    cut = lambda x, t: x[:, t * LANES : (t + 1) * LANES]
+    w = [{k: cut(w[k], t) for k in STEPS} for t in range(2)]
+    keep_own = [cut(keep_own, t) for t in range(2)]
+
+    def pooled(refs, s):
+        z, mid = [], []
+        for t in range(2):
+            rows = three(refs[t], s)
+            mid.append(rows[1])
+            z.append(columns(w[t], *rows))
+        r = [lroll(z[t][0], 1) for t in range(2)]
+        l = [lroll(z[t][2], -1) for t in range(2)]
+        r[1] = jnp.where(head_lane, r[0], r[1])
+        l[0] = jnp.where(tail_lane, l[1], l[0])
+        return [z[t][1] + (r[t] + l[t]) for t in range(2)], mid
+
+    def finish(b, s, pair, sums):
+        j = b * UNROLL + s
+        pair, sums = list(pair), list(sums)
+        if last:
+            group = s % PER
+            row = pl.multiple_of((b * (UNROLL // PER) + s // PER + 1) * SUB, SUB)
+            strip = st[pl.ds(row, SUB), :]
+            pair[0] = jnp.where(lane < 4, lroll(strip, -(GROUP * group + 4)), pair[0])
+            pair[1] = jnp.where(lane >= LANES - 4, lroll(strip, 100 - GROUP * group), pair[1])
+            out = jnp.concatenate(pair, axis=1) * (1.0 / LOG2E)
+            vol_ref[D - 1 - j] = out.astype(jnp.bfloat16)
+            level = (D - 1 - j).astype(jnp.float32) * (1.0 / D)
+        for t in range(2):
+            if not last:
+                v[t, pl.ds(pl.multiple_of((j + 1) * SUB, SUB), SUB), :] = pair[t]
+            e = jnp.exp2(pair[t])
+            sums[2 * t] += e
+            sums[2 * t + 1] += e * (level if last else e)
+        return sums
+
+    def advance(refs, b, s, carry):
+        p_prev, s_prev, v_prev, acc = carry
+        p, mid = pooled(refs, s)
+        s_now = [p_prev[t] + p[t] for t in range(2)]
+        new = [keep_own[t] * v_prev[t] + (s_prev[t] + s_now[t]) for t in range(2)]
+        before = (b - 1, UNROLL - 1) if s == 0 else (b, s - 1)
+        return p, s_now, mid, finish(*before, new, acc)
+
+    def block_refs(b):
+        at = pl.ds(pl.multiple_of(b * (UNROLL * SUB), SUB), (UNROLL + 2) * SUB)
+        return [v.at[t, at, :] for t in range(2)]
+
+    def loop(b, carry):
+        p, s, m, acc = carry
+        carry = list(p), list(s), list(m), list(acc)
+        refs = block_refs(b)
+        for k in range(UNROLL):
+            carry = advance(refs, b, k, carry)
+        return tuple(tuple(c) for c in carry)
+
+    refs = block_refs(0)
+    p, mid = pooled(refs, 0)
+    carry = p, [2.0 * x for x in p], mid, [none] * 4
+    for k in range(1, UNROLL):
+        carry = advance(refs, jnp.int32(0), k, carry)
+    carry = tuple(tuple(c) for c in carry)
+    p_prev, s_prev, v_prev, acc = lax.fori_loop(1, D // UNROLL, loop, carry)
+    new = [keep_own[t] * v_prev[t] + (s_prev[t] + 2.0 * p_prev[t]) for t in range(2)]
+    return tuple(finish(jnp.int32(D // UNROLL - 1), UNROLL - 1, new, acc))
+
+
 def kernel(
-    n, left_ref, right_ref, offs_ref, mask_ref, disp_ref, vol_ref,
-    prev, lf, rs, t4, u, v, own, sent, from_left, from_right, st, w_ref, send_sem, recv_sem,
+    n, left_ref, right_ref, offs_ref, mask_ref, v, st, w_ref, sums_ref,
+    prev, lf, rs, t4, u, own, sent, from_left, from_right, send_sem, recv_sem,
 ):
     channels = left_ref.shape[0]
     tile = left_ref.shape[2]
@@ -147,7 +226,17 @@
         lf[1, at, :] = plane[:, LANES:]
         return tuple(s + d for s, d in zip(sums, distances(plane)))
 
-    weights = affinity(lax.fori_loop(0, channels, channel, (zero,) * 5), channels)
+    per = CHANNEL_UNROLL
+
+    def unrolled(body):
+        def run(i, carry):
+            for k in range(per):
+                carry = body(i * per + k, carry)
+            return carry
+
+        return run
+
+    weights = affinity(lax.fori_loop(0, channels // per, unrolled(channel), (zero,) * 5), channels)
     for i, k in enumerate(STEPS):
         w_ref[i] = weights[k]
 
@@ -181,7 +270,7 @@
                 rs[s, t, at, :] = value
         return carry
 
-    lax.fori_loop(0, channels, shifts, 0)
+    lax.fori_loop(0, channels // per, unrolled(shifts), 0)
 
     depth = 8 * channels
     keep = (iota((depth, tile), 0) // channels == iota((depth, tile), 1) % 8).astype(jnp.bfloat16)
@@ -266,81 +355,9 @@
     def _():
         strip_left.start()
 
-    head_lane, tail_lane = lane == 0, lane == LANES - 1
-
-    def step(sums, last):
-        wide = lambda a, b: jnp.concatenate([a, b], axis=1)
-        w, keep_own = coefficients(
-            {k: w_ref[i] for i, k in enumerate(STEPS)}, usable,
-            wide(sums[0], sums[2]), wide(sums[1], sums[3]),
-        )
-        cut = lambda x, t: x[:, t * LANES : (t + 1) * LANES]
-        w = [{k: cut(w[k], t) for k in STEPS} for t in range(2)]
-        keep_own = [cut(keep_own, t) for t in range(2)]
-
-        def pooled(refs, s):
-            z, mid = [], []
-            for t in range(2):
-                rows = three(refs[t], s)
-                mid.append(rows[1])
-                z.append(columns(w[t], *rows))
-            r = [lroll(z[t][0], 1) for t in range(2)]
-            l = [lroll(z[t][2], -1) for t in range(2)]
-            r[1] = jnp.where(head_lane, r[0], r[1])
-            l[0] = jnp.where(tail_lane, l[1], l[0])
-            return [z[t][1] + (r[t] + l[t]) for t in range(2)], mid
-
-        def finish(b, s, pair, sums):
-            j = b * UNROLL + s
-            pair, sums = list(pair), list(sums)
-            if last:
-                group = s % PER
-                row = pl.multiple_of((b * (UNROLL // PER) + s // PER + 1) * SUB, SUB)
-                strip = st[pl.ds(row, SUB), :]
-                pair[0] = jnp.where(lane < 4, lroll(strip, -(GROUP * group + 4)), pair[0])
-                pair[1] = jnp.where(lane >= LANES - 4, lroll(strip, 100 - GROUP * group), pair[1])
-                out = jnp.concatenate(pair, axis=1) * (1.0 / LOG2E)
-                vol_ref[D - 1 - j] = out.astype(jnp.bfloat16)
-                level = (D - 1 - j).astype(jnp.float32) * (1.0 / D)
-            for t in range(2):
-                if not last:
-                    v[t, pl.ds(pl.multiple_of((j + 1) * SUB, SUB), SUB), :] = pair[t]
-                e = jnp.exp2(pair[t])
-                sums[2 * t] += e
-                sums[2 * t + 1] += e * (level if last else e)
-            return sums
-
-        def advance(refs, b, s, carry):
-            p_prev, s_prev, v_prev, acc = carry
-            p, mid = pooled(refs, s)
-            s_now = [p_prev[t] + p[t] for t in range(2)]
-            new = [keep_own[t] * v_prev[t] + (s_prev[t] + s_now[t]) for t in range(2)]
-            before = (b - 1, UNROLL - 1) if s == 0 else (b, s - 1)
-            return p, s_now, mid, finish(*before, new, acc)
-
-        def block_refs(b):
-            at = pl.ds(pl.multiple_of(b * (UNROLL * SUB), SUB), (UNROLL + 2) * SUB)
-            return [v.at[t, at, :] for t in range(2)]
-
-        def loop(b, carry):
-            p, s, m, acc = carry
-            carry = list(p), list(s), list(m), list(acc)
-            refs = block_refs(b)
-            for k in range(UNROLL):
-                carry = advance(refs, b, k, carry)
-            return tuple(tuple(c) for c in carry)
-
-        refs = block_refs(0)
-        p, mid = pooled(refs, 0)
-        carry = p, [2.0 * x for x in p], mid, [none] * 4
-        for k in range(1, UNROLL):
-            carry = advance(refs, jnp.int32(0), k, carry)
-        carry = tuple(tuple(c) for c in carry)
-        p_prev, s_prev, v_prev, acc = lax.fori_loop(1, D // UNROLL, loop, carry)
-        new = [keep_own[t] * v_prev[t] + (s_prev[t] + 2.0 * p_prev[t]) for t in range(2)]
-        return tuple(finish(jnp.int32(D // UNROLL - 1), UNROLL - 1, new, acc))
-
-    sums = lax.fori_loop(0, ITERS - 1, lambda i, s: step(s, False), sums)
+    sums = lax.fori_loop(
+        0, ITERS - 1, lambda i, s: step(v, st, w_ref, usable, None, s), sums
+    )
 
     @pl.when(has_left)
     def _():
@@ -421,18 +438,24 @@
 
     lax.fori_loop(0, ITERS, strip_step, (s1, s2))
 
-    out = step(sums, True)
+    for t in range(4):
+        sums_ref[t] = sums[t]
+
+    @pl.when(has_right)
+    def _():
+        tile_copy.wait_send()
+        strip_right.wait_send()
+
+    @pl.when(has_left)
+    def _():
+        strip_left.wait_send()
+
+
+def last_kernel(mask_ref, v, st, w_ref, sums_ref, disp_ref, vol_ref):
+    usable = mask_ref[...].astype(jnp.float32)
+    out = step(v, st, w_ref, usable, vol_ref, [sums_ref[t] for t in range(4)])
     for t in range(2):
         disp_ref[:, t * LANES : (t + 1) * LANES] = out[2 * t + 1] / out[2 * t]
-
-    @pl.when(has_right)
-    def _():
-        tile_copy.wait_send()
-        strip_right.wait_send()
-
-    @pl.when(has_left)
-    def _():
-        strip_left.wait_send()
 
 
 def on_device(n, left_features, right_features, tile_offsets, valid_mask):
@@ -440,32 +463,43 @@
     vmem = pl.BlockSpec(memory_space=pltpu.VMEM)
     strips = -(-(BLOCKS + channels // PER + 1) // 4) * 4
     f32 = jnp.float32
-    return pl.pallas_call(
+    state = pl.pallas_call(
         functools.partial(kernel, n),
         out_shape=(
-            jax.ShapeDtypeStruct((rows, tile), f32),
-            jax.ShapeDtypeStruct((D, rows, tile), jnp.bfloat16),
+            jax.ShapeDtypeStruct((2, (D + 2) * SUB, LANES), f32),
+            jax.ShapeDtypeStruct(((BLOCKS + 2) * SUB, LANES), f32),
+            jax.ShapeDtypeStruct((len(STEPS), SUB, tile), f32),
+            jax.ShapeDtypeStruct((4, SUB, LANES), f32),
         ),
         in_specs=[vmem, vmem, pl.BlockSpec(memory_space=pltpu.SMEM), vmem],
-        out_specs=(vmem, vmem),
+        out_specs=(vmem,) * 4,
         scratch_shapes=[
             pltpu.VMEM((channels, rows, tile), jnp.bfloat16),
             pltpu.VMEM((2, channels * SUB, LANES), f32),
             pltpu.VMEM((4, 4, channels * SUB, LANES), f32),
             pltpu.VMEM((ROW_UNROLL, 2 * tile, LANES), f32),
             pltpu.VMEM((2, SUB * PITCH, LANES), f32),
-            pltpu.VMEM((2, (D + 2) * SUB, LANES), f32),
             pltpu.VMEM((strips, SUB, LANES), f32),
             pltpu.VMEM((strips // 4, SUB, LANES), f32),
             pltpu.VMEM((strips // 4, SUB, LANES), f32),
             pltpu.VMEM((strips // 4, SUB, LANES), f32),
-            pltpu.VMEM(((BLOCKS + 2) * SUB, LANES), f32),
-            pltpu.VMEM((len(STEPS), SUB, tile), f32),
             pltpu.SemaphoreType.DMA((3,)),
             pltpu.SemaphoreType.DMA((3,)),
         ],
-        compiler_params=pltpu.CompilerParams(collective_id=0, has_side_effects=True),
+        compiler_params=pltpu.CompilerParams(
+            collective_id=0, has_side_effects=True, vmem_limit_bytes=VMEM_LIMIT
+        ),
     )(left_features, right_features, tile_offsets, valid_mask)
+    return pl.pallas_call(
+        last_kernel,
+        out_shape=(
+            jax.ShapeDtypeStruct((rows, tile), f32),
+            jax.ShapeDtypeStruct((D, rows, tile), jnp.bfloat16),
+        ),
+        in_specs=[vmem] * 5,
+        out_specs=(vmem, vmem),
+        compiler_params=pltpu.CompilerParams(vmem_limit_bytes=VMEM_LIMIT),
+    )(valid_mask, *state)
 
 
 def solution(mesh):

time: 24.8 us -> 21.1 us (0.85)
  Pallas kernels: 19.9 us -> 17.1 us
  local copies, waits for them, and re-layouts: 3.36 us -> 2.5 us
    pallas_call x1, Pallas kernels: 19.9 us -> 14.6 us  [on_device(): pl.pallas_call(functools.partial(kernel, n), out_shape=(jax.ShapeDtypeStr...]
    pallas_call x0 -> x1, Pallas kernels: none -> 2.51 us  [on_device(): pl.pallas_call(last_kernel, out_shape=(jax.ShapeDtypeStruct((rows, tile),...]
    unnamed x2 -> x6, local copies, waits for them, and re-layouts: 3.36 us -> 2.5 us
where the time goes in v3:
time: 21.1 us; the launch traced here: 20.9 us
  Pallas kernels  17.1 us (81%)
  local copies, waits for them, and re-layouts  2.5 us (12%)
  between operations  1.29 us (6%)
    pallas_call x1, Pallas kernels, on_device(): pl.pallas_call(functools.partial(kernel, n), out_shape=(jax.ShapeDtypeStr...  14.6 us
    pallas_call x1, Pallas kernels, on_device(): pl.pallas_call(last_kernel, out_shape=(jax.ShapeDtypeStruct((rows, tile),...  2.51 us
    unnamed x6, local copies, waits for them, and re-layouts  2.5 us

profile of v3, /device:TPU:24, one launch (start us, length us, event | category | flops | bytes accessed | tf_op | source)
XLA Modules:
  0.0 20.9 jit_solution(10613558481157024928)
XLA Ops:
  1.3 0.0 copy-start
  1.3 0.9 %copy-done = bf16[32,8,256]{2,1,0:T(8,128)(2,1)S(1)} copy-done((bf16[32,8,256]{2,1,0:T(8,128)(2,1)S(1)}, bf16[32,8,256]{2,1,0:T(8,128)(2,1)}, u32[]{:S(2)}) %copy-start) | copy-done | bytes 131096
  2.2 0.0 copy-start.1
  2.2 0.9 %copy-done.1 = bf16[32,8,256]{2,1,0:T(8,128)(2,1)S(1)} copy-done((bf16[32,8,256]{2,1,0:T(8,128)(2,1)S(1)}, bf16[32,8,256]{2,1,0:T(8,128)(2,1)}, u32[]{:S(2)}) %copy-start.1) | copy-done | bytes 131096
  3.1 0.0 copy-start.2
  3.1 0.7 %copy-done.2 = s32[8,256]{1,0:T(8,128)S(1)} copy-done((s32[8,256]{1,0:T(8,128)S(1)}, s32[8,256]{1,0:T(8,128)}, u32[]{:S(2)}) %copy-start.2) | copy-done | bytes 8216
  3.8 14.6 %shard_map.59 = (f32[2,1552,128]{2,1,0:T(8,128)S(1)}, f32[400,128]{1,0:T(8,128)S(1)}, f32[9,8,256]{2,1,0:T(8,128)S(1)}, f32[4,8,128]{2,1,0:T(8,128)S(1)}) custom-call(bf16[32,8,256]{2,1,0:T(8,128)(2,1)S(1)} %copy-done, bf16[32,8,256]{2,1,0:T(8,128)(2,1)S(1)} %copy-done.1, s32[1]{0:T(128)S(6)} %copy.6.offs_ref, s32[8,256]{1,0:T(8,128)S(1)} %copy-done.2), custom_call_target="tpu_custom_call" | custom-call | tf_op jit(solution)/shard_map/pallas_call | solution.py:466
  18.4 2.5 %shard_map.60 = (f32[8,256]{1,0:T(8,128)}, bf16[192,8,256]{2,1,0:T(8,128)(2,1)}) custom-call(s32[8,256]{1,0:T(8,128)S(1)} %copy-done.2, f32[2,1552,128]{2,1,0:T(8,128)S(1)} %get-tuple-element.6.v, f32[400,128]{1,0:T(8,128)S(1)} %get-tuple-element.7.st, f32[9,8,256]{2,1,0:T(8,128)S(1)} %get-tuple-element.8.w_ref, f32[4,8,128]{2,1,0:T(8,128)S(1)} %get-tuple-element.9.sums_ref), custom_call_target="tpu_custom_call" | custom-call | tf_op jit(solution)/shard_map/pallas_call | solution.py:493
Async XLA Ops:
  1.3 0.9 %copy-start = (bf16[32,8,256]{2,1,0:T(8,128)(2,1)S(1)}, bf16[32,8,256]{2,1,0:T(8,128)(2,1)}, u32[]{:S(2)}) copy-start(bf16[32,8,256]{2,1,0:T(8,128)(2,1)} %left_ref.1) | copy-start | bytes 393220
  2.2 0.9 %copy-start.1 = (bf16[32,8,256]{2,1,0:T(8,128)(2,1)S(1)}, bf16[32,8,256]{2,1,0:T(8,128)(2,1)}, u32[]{:S(2)}) copy-start(bf16[32,8,256]{2,1,0:T(8,128)(2,1)} %right_ref.1) | copy-start | bytes 393220
  3.1 0.7 %copy-start.2 = (s32[8,256]{1,0:T(8,128)S(1)}, s32[8,256]{1,0:T(8,128)}, u32[]{:S(2)}) copy-start(s32[8,256]{1,0:T(8,128)} %mask_ref.3) | copy-start | bytes 24580

commit v4 on v3

--- a/solution.py
+++ b/solution.py
@@ -21,10 +21,10 @@
 BLOCKS = D // PER
 LOG2E = math.log2(math.e)
 FIRST_UNROLL = 48
-UNROLL = 96
+UNROLL = 192
 STRIP_UNROLL = 48
-ROW_UNROLL = 4
-CHANNEL_UNROLL = 8
+ROW_UNROLL = 8
+CHANNEL_UNROLL = 32
 VMEM_LIMIT = 24 * 1024 * 1024
 
 

time: 21.1 us -> 20.7 us (0.981)
  Pallas kernels: 17.1 us -> 16.7 us
    pallas_call x1, Pallas kernels: 14.6 us -> 14.2 us  [on_device(): pl.pallas_call(functools.partial(kernel, n), out_shape=(jax.ShapeDtypeStr...]
where the time goes in v4:
time: 20.7 us; the launch traced here: 20.5 us
  Pallas kernels  16.7 us (81%)
  local copies, waits for them, and re-layouts  2.5 us (12%)
  between operations  1.29 us (6%)
    pallas_call x1, Pallas kernels, on_device(): pl.pallas_call(functools.partial(kernel, n), out_shape=(jax.ShapeDtypeStr...  14.2 us
    pallas_call x1, Pallas kernels, on_device(): pl.pallas_call(last_kernel, out_shape=(jax.ShapeDtypeStruct((rows, tile),...  2.51 us
    unnamed x6, local copies, waits for them, and re-layouts  2.5 us

profile of v4, /device:TPU:24, one launch (start us, length us, event | category | flops | bytes accessed | tf_op | source)
XLA Modules:
  0.0 20.5 jit_solution(1035114664671544416)
XLA Ops:
  1.3 0.0 copy-start
  1.3 0.9 %copy-done = bf16[32,8,256]{2,1,0:T(8,128)(2,1)S(1)} copy-done((bf16[32,8,256]{2,1,0:T(8,128)(2,1)S(1)}, bf16[32,8,256]{2,1,0:T(8,128)(2,1)}, u32[]{:S(2)}) %copy-start) | copy-done | bytes 131096
  2.2 0.0 copy-start.1
  2.2 0.9 %copy-done.1 = bf16[32,8,256]{2,1,0:T(8,128)(2,1)S(1)} copy-done((bf16[32,8,256]{2,1,0:T(8,128)(2,1)S(1)}, bf16[32,8,256]{2,1,0:T(8,128)(2,1)}, u32[]{:S(2)}) %copy-start.1) | copy-done | bytes 131096
  3.1 0.0 copy-start.2
  3.1 0.7 %copy-done.2 = s32[8,256]{1,0:T(8,128)S(1)} copy-done((s32[8,256]{1,0:T(8,128)S(1)}, s32[8,256]{1,0:T(8,128)}, u32[]{:S(2)}) %copy-start.2) | copy-done | bytes 8216
  3.8 14.2 %shard_map.59 = (f32[2,1552,128]{2,1,0:T(8,128)S(1)}, f32[400,128]{1,0:T(8,128)S(1)}, f32[9,8,256]{2,1,0:T(8,128)S(1)}, f32[4,8,128]{2,1,0:T(8,128)S(1)}) custom-call(bf16[32,8,256]{2,1,0:T(8,128)(2,1)S(1)} %copy-done, bf16[32,8,256]{2,1,0:T(8,128)(2,1)S(1)} %copy-done.1, s32[1]{0:T(128)S(6)} %copy.6.offs_ref, s32[8,256]{1,0:T(8,128)S(1)} %copy-done.2), custom_call_target="tpu_custom_call" | custom-call | tf_op jit(solution)/shard_map/pallas_call | solution.py:466
  17.9 2.5 %shard_map.60 = (f32[8,256]{1,0:T(8,128)}, bf16[192,8,256]{2,1,0:T(8,128)(2,1)}) custom-call(s32[8,256]{1,0:T(8,128)S(1)} %copy-done.2, f32[2,1552,128]{2,1,0:T(8,128)S(1)} %get-tuple-element.6.v, f32[400,128]{1,0:T(8,128)S(1)} %get-tuple-element.7.st, f32[9,8,256]{2,1,0:T(8,128)S(1)} %get-tuple-element.8.w_ref, f32[4,8,128]{2,1,0:T(8,128)S(1)} %get-tuple-element.9.sums_ref), custom_call_target="tpu_custom_call" | custom-call | tf_op jit(solution)/shard_map/pallas_call | solution.py:493
Async XLA Ops:
  1.3 0.9 %copy-start = (bf16[32,8,256]{2,1,0:T(8,128)(2,1)S(1)}, bf16[32,8,256]{2,1,0:T(8,128)(2,1)}, u32[]{:S(2)}) copy-start(bf16[32,8,256]{2,1,0:T(8,128)(2,1)} %left_ref.1) | copy-start | bytes 393220
  2.2 0.9 %copy-start.1 = (bf16[32,8,256]{2,1,0:T(8,128)(2,1)S(1)}, bf16[32,8,256]{2,1,0:T(8,128)(2,1)}, u32[]{:S(2)}) copy-start(bf16[32,8,256]{2,1,0:T(8,128)(2,1)} %right_ref.1) | copy-start | bytes 393220
  3.1 0.7 %copy-start.2 = (s32[8,256]{1,0:T(8,128)S(1)}, s32[8,256]{1,0:T(8,128)}, u32[]{:S(2)}) copy-start(s32[8,256]{1,0:T(8,128)} %mask_ref.3) | copy-start | bytes 24580
